TPU v7x, 128 devices: a whole 4x4x4 slice. The times are simulated.
128 devices in a mesh: slot: 32 (over z, y, x_hi), row: 2 (over core), col: 2 (over x_lo).
Axes of the slice: x: 4 (x_hi: 2, x_lo: 2; x = x_hi * 2 + x_lo), y: 4, z: 4, core: 2. Of those that a mesh axis runs over, the one named last changes fastest.
Arguments:
- hidden: bfloat16 [32, 128, 4096], P('slot', None, 'row'), may hold values from -20 to 20
- w_query: bfloat16 [4096, 4096], P('row', 'col'), may hold values from -0.09375 to 0.09375
- key_weight: bfloat16 [4096, 1024], P('row', 'col'), may hold values from -0.09375 to 0.09375
- value_weight: bfloat16 [4096, 1024], P('row', 'col'), may hold values from -0.09375 to 0.09375
- w_out: bfloat16 [4096, 4096], P('col', 'row'), may hold values from -0.09375 to 0.09375
- kv_store: bfloat16 [8192, 2, 8, 1024], P(('slot', 'row'), None, None, 'col'), may hold values from -250 to 250
- stretch_offset: int32 [8192], replicated, may hold values from 0 to 4095
- tile_stretch: int32 [32, 256], replicated, may hold values from 0 to 8191, as said below
- slot_count: int32 [32], replicated, may hold values from 160 to 256, as said below
- recomp_pos: int32 [32, 128], P('slot'), may hold values from 0 to 2047, as said below
Outputs:
- attn_out: bfloat16 [32, 128, 4096], P('slot', 'col', 'row')
Inputs may be any that keep to these rules, and one draw needn't show every extreme that they name: Within each aligned block of 128 tiles of a slot, every value of tile_stretch // 128 that occurs occurs exactly 2 times, and 64 distinct such values occur. `slot_count`: one slot uses all 256 tiles. `recomp_pos`: entry i of slot s lies in [i * q, (i + 1) * q) with q = slot_count[s] * 8 // 128.
All inputs are finite; a program needn't handle non-finite values.
Results may differ from a plain program's by a relative error of at most 0.018.
The roundings to bfloat16 on the way count: a program that leaves them out, or rounds other values in their place, can miss the bound.
Values may be sent and summed in bfloat16 or wider, within the bound.
A program may use at most 128 MiB of HBM per device.

v0:
```python
import math

import jax
import jax.numpy as jnp
from jax import lax
from jax.sharding import PartitionSpec as P

HEAD_WIDTH = 128


NEGATIVE = -1e30
ROPE_BASE = 500000.0


def joined(value, axis, join):
    pieces = jax.tree.map(lambda part: lax.all_gather(part, axis), value)
    head = jax.tree.map(lambda part: part[0], pieces)
    tail = jax.tree.map(lambda part: part[1:], pieces)
    running, _ = lax.scan(lambda running, piece: (join(running, piece), None), head, tail)
    return running


def frequencies(head_size):
    freq_index = jnp.arange(head_size // 2, dtype=jnp.float32)
    return ROPE_BASE ** (-2.0 * freq_index / head_size)


def apply_rotation(vectors, angles):
    half_dim = vectors.shape[-1] // 2
    front_half = vectors[..., :half_dim]
    back_half = vectors[..., half_dim:]
    cosine_part = jnp.cos(angles)
    sine_part = jnp.sin(angles)
    return jnp.concatenate(
        [
            front_half * cosine_part - back_half * sine_part,
            back_half * cosine_part + front_half * sine_part,
        ],
        axis=-1,
    )


def combine_partials(first, second):
    peak_score = jnp.maximum(first[0], second[0])
    left_scale = jnp.exp(first[0] - peak_score)
    right_scale = jnp.exp(second[0] - peak_score)
    return (
        peak_score,
        first[1] * left_scale + second[1] * right_scale,
        first[2] * left_scale[..., None] + second[2] * right_scale[..., None],
    )


def on_device(
    hidden,
    w_query,
    key_weight,
    value_weight,
    w_out,
    kv_store,
    stretch_offset,
    tile_stretch,
    slot_count,
    recomp_pos,
):
    slot_total = lax.axis_size("slot")
    row_total = lax.axis_size("row")
    peer_count = slot_total * row_total
    tile_count = kv_store.shape[0]
    stretch_len = kv_store.shape[2]
    key_value_columns = kv_store.shape[3]
    head_size = HEAD_WIDTH
    kv_heads = key_value_columns // head_size
    query_columns = w_query.shape[1]
    q_heads = query_columns // head_size
    queries_per_key_head = q_heads // kv_heads
    capacity = max(2, tile_count // peer_count)
    rsel_rows = hidden.shape[1]
    row_share = rsel_rows // row_total
    slot_index = lax.axis_index("slot")
    row_index = lax.axis_index("row")
    own_index = slot_index * row_total + row_index
    freq_table = frequencies(head_size)
    tile_ids = jnp.arange(tile_stretch.shape[1], dtype=jnp.int32)
    valid_all = (tile_ids[None, :] < slot_count[:, None]).reshape(peer_count, tile_count)
    stretches_all = tile_stretch.reshape(peer_count, tile_count)
    is_mine = jnp.logical_and(stretches_all // tile_count == own_index, valid_all).astype(jnp.int32)
    slot_rank = jnp.cumsum(is_mine, axis=1) - 1
    capacity_ids = jnp.arange(capacity, dtype=jnp.int32)
    select = is_mine[:, None, :] * (slot_rank[:, None, :] == capacity_ids[None, :, None]).astype(
        jnp.int32
    )
    local_ids = jnp.sum(select * (stretches_all % tile_count)[:, None, :], axis=2)
    present = jnp.sum(select, axis=2) > 0
    outgoing = jnp.take(kv_store, local_ids.reshape(-1), axis=0)
    outgoing = jnp.where(
        present.reshape(-1)[:, None, None, None], outgoing, jnp.zeros((), kv_store.dtype)
    )
    outgoing = outgoing.reshape(peer_count, capacity, 2, stretch_len, key_value_columns)
    incoming = lax.all_to_all(outgoing, ("slot", "row"), split_axis=0, concat_axis=0, tiled=True)
    incoming = incoming.reshape(peer_count * capacity, 2, stretch_len, key_value_columns)
    weights = jnp.concatenate([w_query, key_weight, value_weight], axis=1)
    tokens = hidden[0]
    row_block = tokens
    projected_rows = lax.psum_scatter(
        jnp.dot(row_block, weights, preferred_element_type=jnp.float32),
        "row",
        scatter_dimension=0,
        tiled=True,
    )
    positions = recomp_pos[0]
    own_pos = lax.dynamic_slice_in_dim(positions, row_index * row_share, row_share)
    token_angle = own_pos.astype(jnp.float32)[:, None, None] * freq_table
    queries = (
        apply_rotation(
            projected_rows[:, :query_columns].reshape(row_share, q_heads, head_size), token_angle
        )
        .astype(jnp.bfloat16)
        .reshape(row_share, query_columns)
    )
    fresh_keys = (
        apply_rotation(
            projected_rows[:, query_columns : query_columns + key_value_columns].reshape(
                row_share, kv_heads, head_size
            ),
            token_angle,
        )
        .astype(jnp.bfloat16)
        .reshape(row_share, key_value_columns)
    )
    new_values = projected_rows[:, query_columns + key_value_columns :].astype(jnp.bfloat16)
    queries, fresh_keys, new_values = (
        lax.all_gather(queries, "row", axis=0, tiled=True),
        lax.all_gather(fresh_keys, "row", axis=0, tiled=True),
        lax.all_gather(new_values, "row", axis=0, tiled=True),
    )
    base_tile = row_index * tile_count
    my_stretches = lax.dynamic_slice_in_dim(tile_stretch[slot_index], base_tile, tile_count)
    my_count = slot_count[slot_index]
    local_tiles = jnp.arange(tile_count, dtype=jnp.int32)
    my_valid = base_tile + local_tiles < my_count
    owners = my_stretches // tile_count
    earlier = jnp.logical_and(
        owners[None, :] == owners[:, None], local_tiles[None, :] < local_tiles[:, None]
    )
    earlier = jnp.logical_and(earlier, my_valid[None, :])
    my_rank = jnp.sum(earlier.astype(jnp.int32), axis=1)
    landing_slot = jnp.where(my_valid, owners * capacity + jnp.minimum(my_rank, capacity - 1), 0)
    arrived = jnp.take(incoming, landing_slot, axis=0)
    key_shift = (base_tile + local_tiles) * stretch_len - jnp.take(stretch_offset, my_stretches)
    key_angle = key_shift.astype(jnp.float32)[:, None, None, None] * freq_table
    unrotated_keys = (
        arrived[:, 0].astype(jnp.float32).reshape(tile_count, stretch_len, kv_heads, head_size)
    )
    local_keys = tile_count * stretch_len
    joined_keys = (
        apply_rotation(unrotated_keys, key_angle)
        .astype(jnp.bfloat16)
        .reshape(local_keys, key_value_columns)
    )
    joined_values = arrived[:, 1].reshape(local_keys, key_value_columns)
    key_base = base_tile * stretch_len
    landing = positions - key_base
    inside = jnp.logical_and(landing >= 0, landing < local_keys)
    landing = jnp.where(inside, landing, local_keys)
    joined_keys = joined_keys.at[landing].set(fresh_keys, mode="drop")
    joined_values = joined_values.at[landing].set(new_values, mode="drop")
    key_span = min(256, local_keys)
    span_count = local_keys // key_span
    grouped = queries.reshape(rsel_rows, kv_heads, queries_per_key_head, head_size)
    length_limit = my_count * stretch_len
    score_scale = 1.0 / math.sqrt(head_size)

    def attend(carry, span_index):
        running_max, weight_sum, weighted = carry
        span_start = span_index * key_span
        key_block = lax.dynamic_slice_in_dim(joined_keys, span_start, key_span, 0).reshape(
            key_span, kv_heads, head_size
        )
        value_block = lax.dynamic_slice_in_dim(joined_values, span_start, key_span, 0).reshape(
            key_span, kv_heads, head_size
        )
        scores = (
            jnp.einsum("qgjd,kgd->qgjk", grouped, key_block, preferred_element_type=jnp.float32)
            * score_scale
        )
        key_pos = key_base + span_start + jnp.arange(key_span, dtype=jnp.int32)
        allowed = jnp.logical_and(
            key_pos[None, :] <= positions[:, None], key_pos[None, :] < length_limit
        )[:, None, None, :]
        scores = jnp.where(allowed, scores, NEGATIVE)
        peak_score = jnp.maximum(running_max, jnp.max(scores, axis=3))
        probs = jnp.where(allowed, jnp.exp(scores - peak_score[..., None]), 0.0)
        factor = jnp.exp(running_max - peak_score)
        weight_sum = weight_sum * factor + jnp.sum(probs, axis=3)
        weighted = weighted * factor[..., None] + jnp.einsum(
            "qgjk,kgd->qgjd",
            probs.astype(jnp.bfloat16),
            value_block,
            preferred_element_type=jnp.float32,
        )
        return ((peak_score, weight_sum, weighted), None)

    start_max = jnp.full((rsel_rows, kv_heads, queries_per_key_head), NEGATIVE, jnp.float32)
    start_sum = jnp.zeros((rsel_rows, kv_heads, queries_per_key_head), jnp.float32)
    start_weighted = jnp.zeros((rsel_rows, kv_heads, queries_per_key_head, head_size), jnp.float32)
    (running_max, weight_sum, weighted), _ = lax.scan(
        attend, (start_max, start_sum, start_weighted), jnp.arange(span_count, dtype=jnp.int32)
    )
    running_max, weight_sum, weighted = joined(
        (running_max, weight_sum, weighted), "row", combine_partials
    )
    attended = (
        (weighted / weight_sum[..., None]).astype(jnp.bfloat16).reshape(rsel_rows, query_columns)
    )
    row_block = attended
    result = lax.psum_scatter(
        jnp.dot(row_block, w_out, preferred_element_type=jnp.float32).astype(jnp.bfloat16),
        "col",
        scatter_dimension=0,
        tiled=True,
    )
    return result[None]


def solution(mesh):
    return jax.shard_map(
        on_device,
        mesh=mesh,
        in_specs=(
            P("slot", None, "row"),
            P("row", "col"),
            P("row", "col"),
            P("row", "col"),
            P("col", "row"),
            P(("slot", "row"), None, None, "col"),
            P(),
            P(),
            P(),
            P("slot", None),
        ),
        out_specs=P("slot", "col", "row"),
        check_vma=False,
    )
```

profile of v0, /device:TPU:1, one launch (start us, length us, event | category | flops | bytes accessed | tf_op | source)
XLA Modules:
  0.0 167.9 jit_solution(17775547539881789211)
XLA Ops:
  6.5 0.9 reshape.542
  7.5 0.7 lt.136
  9.4 2.0 %gather_fusion.1 = bf16[128,2,8,512]{3,2,1,0:T(8,128)(2,1)} fusion(bf16[128,2,8,512]{3,2,1,0:T(8,128)(2,1)S(1)} %copy-done, s32[1024]{0:T(1024)S(1)} %pad_clamp_fusion.2), kind=kCustom, calls=%fused_computation.clone | custom fusion | bytes 4194816 | tf_op jit(solution)/shard_map/jit(_take)/gather | solution.py:95
  11.4 3.0 %select_select_fusion = bf16[128,2,8,512]{3,2,1,0:T(8,128)(2,1)} fusion(bf16[128,2,8,512]{3,2,1,0:T(8,128)(2,1)} %gather_fusion.1, pred[128]{0:T(512)(128)(4,1)S(1)} %compare_and_fusion.2, pred[128]{0:T(512)(128)(4,1)S(1)} %gt.17), kind=kLoop, calls=%fused_computation.38 | loop fusion | flops 2097152 | bytes 4194560 | tf_op jit(solution)/shard_map/jit(_where)/select_n | solution.py:96
  14.4 12.8 %all-to-all-start = ((bf16[64,2,2,8,512]{4,3,2,1,0:T(8,128)(2,1)}), bf16[64,2,2,8,512]{4,3,2,1,0:T(8,128)(2,1)}, u32[]{:S(2)}, u32[]{:S(2)}) async-start(bf16[64,2,2,8,512]{4,3,2,1,0:T(8,128)(2,1)} %bitcast.104), calls=%async_computation | async-start | bytes 4194304 | tf_op jit(solution)/shard_map/all_to_all | solution.py:100
  27.2 8.3 %fusion.20 = f32[128,3072]{0,1:T(8,128)} fusion(bf16[2048,512]{1,0:T(8,128)(2,1)} %param.17, bf16[2048,512]{1,0:T(8,128)(2,1)} %param.16, bf16[2048,2048]{1,0:T(8,128)(2,1)} %param.15, bf16[1,128,2048]{2,1,0:T(8,128)(2,1)S(1)} %copy-done.5), kind=kOutput, calls=%fused_computation.36 | convolution fusion | flops 1648361472 | bytes 14680064 | tf_op jit(solution)/shard_map/dot_general | solution.py:106
  35.5 3.1 %copy.55 = f32[128,3072]{1,0:T(8,128)} copy(f32[128,3072]{0,1:T(8,128)} %fusion.20) | data formatting | bytes 3145728
  38.7 0.8 fusion.38
  40.2 1.1 gather_fusion
  43.0 0.7 compare_and_fusion.1
  44.3 13.9 %all-to-all-done = bf16[64,2,2,8,512]{4,3,2,1,0:T(8,128)(2,1)} async-done(((bf16[64,2,2,8,512]{4,3,2,1,0:T(8,128)(2,1)}), bf16[64,2,2,8,512]{4,3,2,1,0:T(8,128)(2,1)}, u32[]{:S(2)}, u32[]{:S(2)}) %all-to-all-start) | async-done | bytes 2097184 | tf_op jit(solution)/shard_map/all_to_all | solution.py:100
  58.1 3.6 %gather_fusion.2 = bf16[128,2,8,512]{3,2,1,0:T(8,128)(2,1)} fusion(bf16[128,2,8,512]{3,2,1,0:T(8,128)(2,1)} %bitcast.5, s32[1024]{0:T(1024)S(1)} %pad_clamp_fusion.1), kind=kCustom, calls=%fused_computation.1.clone | custom fusion | bytes 4194816 | tf_op jit(solution)/shard_map/jit(_take)/gather | solution.py:149
  61.7 1.9 %broadcast_select_fusion = bf16[128,2,8,512]{3,2,1,0:T(8,128)(2,1)S(1)} fusion(bf16[128,2,8,512]{3,2,1,0:T(8,128)(2,1)} %gather_fusion.2, pred[128]{0:T(512)(128)(4,1)S(1)} %get-tuple-element.200), kind=kLoop, calls=%fused_computation.41 | loop fusion | flops 1048576 | bytes 4194432 | tf_op jit(solution)/shard_map/jit(_take)/select_n | solution.py:149
  63.6 1.3 slice_bitcast_fusion
  64.8 0.8 subtract_convert_fusion
  65.6 1.5 maximum_bitcast_fusion
  67.2 1.0 slice.84
  68.5 2.0 %all_gather.27 = bf16[128,512]{1,0:T(8,128)(2,1)S(1)} all-gather(bf16[64,512]{1,0:T(8,128)(2,1)S(1)} %copy.51), channel_id=1, replica_groups=mesh['slot'=32,'row'=2,'col'=2] {'row'}, dimensions={0}, use_global_device_ids=true | all-gather | bytes 196608 | tf_op jit(solution)/shard_map/all_gather | solution.py:134
  70.5 0.9 slice.91
  71.6 1.9 %all_gather.29 = bf16[128,512]{1,0:T(8,128)(2,1)S(1)} all-gather(bf16[64,512]{1,0:T(8,128)(2,1)S(1)} %copy.44), channel_id=1, replica_groups=mesh['slot'=32,'row'=2,'col'=2] {'row'}, dimensions={0}, use_global_device_ids=true | all-gather | bytes 196608 | tf_op jit(solution)/shard_map/all_gather | solution.py:135
  73.5 0.8 slice.87
  74.3 1.4 copy.60
  76.2 2.2 %all_gather.28 = bf16[128,2048]{1,0:T(8,128)(2,1)S(1)} all-gather(bf16[64,2048]{1,0:T(8,128)(2,1)S(1)} %copy.52), channel_id=1, replica_groups=mesh['slot'=32,'row'=2,'col'=2] {'row'}, dimensions={0}, use_global_device_ids=true | all-gather | bytes 786432 | tf_op jit(solution)/shard_map/all_gather | solution.py:133
  79.0 3.4 %scatter_fusion = bf16[1024,512]{1,0:T(8,128)(2,1)} fusion(bf16[1024,512]{1,0:T(8,128)(2,1)} %maximum_bitcast_fusion, s32[128]{0:T(128)S(1)} %fusion.39, bf16[128,512]{1,0:T(8,128)(2,1)S(1)} %all_gather.27), kind=kCustom, calls=%fused_computation.3 | custom fusion | bytes 393728 | tf_op jit(solution)/shard_map/scatter | solution.py:166
  82.4 3.4 %scatter_fusion.1 = bf16[1024,512]{1,0:T(8,128)(2,1)} fusion(bf16[1024,512]{1,0:T(8,128)(2,1)} %get-tuple-element.208, s32[128]{0:T(128)S(1)} %fusion.39, bf16[128,512]{1,0:T(8,128)(2,1)S(1)} %all_gather.29), kind=kCustom, calls=%fused_computation.4 | custom fusion | bytes 393728 | tf_op jit(solution)/shard_map/scatter | solution.py:167
  85.8 41.1 %while.3 = (s32[]{:T(128)}, f32[128,4,4]{0,2,1:T(4,128)S(1)}, f32[128,4,4]{0,2,1:T(4,128)S(1)}, f32[128,4,4,128]{0,3,2,1:T(8,128)}, s32[4]{0:T(128)S(1)}, /*inde...) while((s32[]{:T(128)}, f32[128,4,4]{0,2,1:T(4,128)S(1)}, ...), condition=%wide.region_10.12_spmd.clone, body=%wide.region_7.11_spmd.clone.sunk | while | flops 276114176 | bytes 11799791 | solution.py:207
  87.1 1.1 constant_dynamic-slice_fusion.3
  88.5 1.9 %fusion.63 = (f32[128,4,4]{0,2,1:T(4,128)S(1)}, f32[4,256,128,4]{2,1,3,0:T(8,128)}) fusion(pred[128,256]{0,1:T(8,128)(4,1)S(1)} %compare_and_fusion.4, bf16[256,4,128,1]{0,2,3,1:T(8,128)(2,1)S(1)} %bitcast.103, bf16[128,4,4,128]{3,0,2,1:T(8,128)(2,1)S(1)} %get-tuple-element.340), kind=kOutput, calls=%fused_computation.7.clone.1 | convolution fusion | flops 135788544 | bytes 2924544 | tf_op jit(solution)/shard_map/while/body/eval_jaxpr/qgjd,kgd->qgjk/dot_general | solution.py:184
  90.4 2.1 %fusion.64 = f32[128,4,4]{0,2,1:T(4,128)S(1)} fusion(f32[4,256,128,4]{2,1,3,0:T(8,128)} %get-tuple-element.297, f32[128,4,4]{0,2,1:T(4,128)S(1)} %select_maximum_fusion.2, pred[128,256]{0,1:T(8,128)(4,1)S(1)} %compare_and_fusion.4), kind=kLoop, calls=%fused_computation.9.clone.1 | loop fusion | flops 2619392 | bytes 2146304 | tf_op jit(solution)/shard_map/while/body/eval_jaxpr/reduce_sum | solution.py:195
  92.7 3.2 %fusion.66 = f32[128,4,4,128]{0,3,2,1:T(8,128)} fusion(bf16[256,4,128,1]{0,2,3,1:T(8,128)(2,1)S(1)} %bitcast.105, f32[4,256,128,4]{2,1,3,0:T(8,128)} %get-tuple-element.297, f32[128,4,4,128]{0,3,2,1:T(8,128)} %get-tuple-element.319, f32[128,4,4]{0,2,1:T(4,128)S(1)} %select_maximum_fusion.2, pred[128,256]{0,1:T(8,128)(4,1)S(1)} %compare_and_fusion.4, ...), kind=kOutput, calls=%fused_computation.11.clone.1 | convolution fusion | flops 137625600 | bytes 4505601 | tf_op jit(solution)/shard_map/while/body/eval_jaxpr/qgjk,kgd->qgjd/dot_general | solution.py:196
  97.2 1.1 constant_dynamic-slice_fusion.3
  98.6 1.9 %fusion.63 = (f32[128,4,4]{0,2,1:T(4,128)S(1)}, f32[4,256,128,4]{2,1,3,0:T(8,128)}) fusion(pred[128,256]{0,1:T(8,128)(4,1)S(1)} %compare_and_fusion.4, bf16[256,4,128,1]{0,2,3,1:T(8,128)(2,1)S(1)} %bitcast.103, bf16[128,4,4,128]{3,0,2,1:T(8,128)(2,1)S(1)} %get-tuple-element.340), kind=kOutput, calls=%fused_computation.7.clone.1 | convolution fusion | flops 135788544 | bytes 2924544 | tf_op jit(solution)/shard_map/while/body/eval_jaxpr/qgjd,kgd->qgjk/dot_general | solution.py:184
  100.5 2.1 %fusion.64 = f32[128,4,4]{0,2,1:T(4,128)S(1)} fusion(f32[4,256,128,4]{2,1,3,0:T(8,128)} %get-tuple-element.297, f32[128,4,4]{0,2,1:T(4,128)S(1)} %select_maximum_fusion.2, pred[128,256]{0,1:T(8,128)(4,1)S(1)} %compare_and_fusion.4), kind=kLoop, calls=%fused_computation.9.clone.1 | loop fusion | flops 2619392 | bytes 2146304 | tf_op jit(solution)/shard_map/while/body/eval_jaxpr/reduce_sum | solution.py:195
  102.7 3.5 %fusion.66 = f32[128,4,4,128]{0,3,2,1:T(8,128)} fusion(bf16[256,4,128,1]{0,2,3,1:T(8,128)(2,1)S(1)} %bitcast.105, f32[4,256,128,4]{2,1,3,0:T(8,128)} %get-tuple-element.297, f32[128,4,4,128]{0,3,2,1:T(8,128)} %get-tuple-element.319, f32[128,4,4]{0,2,1:T(4,128)S(1)} %select_maximum_fusion.2, pred[128,256]{0,1:T(8,128)(4,1)S(1)} %compare_and_fusion.4, ...), kind=kOutput, calls=%fused_computation.11.clone.1 | convolution fusion | flops 137625600 | bytes 4505601 | tf_op jit(solution)/shard_map/while/body/eval_jaxpr/qgjk,kgd->qgjd/dot_general | solution.py:196
  107.6 1.1 constant_dynamic-slice_fusion.3
  109.0 1.9 %fusion.63 = (f32[128,4,4]{0,2,1:T(4,128)S(1)}, f32[4,256,128,4]{2,1,3,0:T(8,128)}) fusion(pred[128,256]{0,1:T(8,128)(4,1)S(1)} %compare_and_fusion.4, bf16[256,4,128,1]{0,2,3,1:T(8,128)(2,1)S(1)} %bitcast.103, bf16[128,4,4,128]{3,0,2,1:T(8,128)(2,1)S(1)} %get-tuple-element.340), kind=kOutput, calls=%fused_computation.7.clone.1 | convolution fusion | flops 135788544 | bytes 2924544 | tf_op jit(solution)/shard_map/while/body/eval_jaxpr/qgjd,kgd->qgjk/dot_general | solution.py:184
  110.8 2.1 %fusion.64 = f32[128,4,4]{0,2,1:T(4,128)S(1)} fusion(f32[4,256,128,4]{2,1,3,0:T(8,128)} %get-tuple-element.297, f32[128,4,4]{0,2,1:T(4,128)S(1)} %select_maximum_fusion.2, pred[128,256]{0,1:T(8,128)(4,1)S(1)} %compare_and_fusion.4), kind=kLoop, calls=%fused_computation.9.clone.1 | loop fusion | flops 2619392 | bytes 2146304 | tf_op jit(solution)/shard_map/while/body/eval_jaxpr/reduce_sum | solution.py:195
  113.1 3.5 %fusion.66 = f32[128,4,4,128]{0,3,2,1:T(8,128)} fusion(bf16[256,4,128,1]{0,2,3,1:T(8,128)(2,1)S(1)} %bitcast.105, f32[4,256,128,4]{2,1,3,0:T(8,128)} %get-tuple-element.297, f32[128,4,4,128]{0,3,2,1:T(8,128)} %get-tuple-element.319, f32[128,4,4]{0,2,1:T(4,128)S(1)} %select_maximum_fusion.2, pred[128,256]{0,1:T(8,128)(4,1)S(1)} %compare_and_fusion.4, ...), kind=kOutput, calls=%fused_computation.11.clone.1 | convolution fusion | flops 137625600 | bytes 4505601 | tf_op jit(solution)/shard_map/while/body/eval_jaxpr/qgjk,kgd->qgjd/dot_general | solution.py:196
  117.9 1.1 constant_dynamic-slice_fusion.3
  119.3 1.9 %fusion.63 = (f32[128,4,4]{0,2,1:T(4,128)S(1)}, f32[4,256,128,4]{2,1,3,0:T(8,128)}) fusion(pred[128,256]{0,1:T(8,128)(4,1)S(1)} %compare_and_fusion.4, bf16[256,4,128,1]{0,2,3,1:T(8,128)(2,1)S(1)} %bitcast.103, bf16[128,4,4,128]{3,0,2,1:T(8,128)(2,1)S(1)} %get-tuple-element.340), kind=kOutput, calls=%fused_computation.7.clone.1 | convolution fusion | flops 135788544 | bytes 2924544 | tf_op jit(solution)/shard_map/while/body/eval_jaxpr/qgjd,kgd->qgjk/dot_general | solution.py:184
  121.2 2.1 %fusion.64 = f32[128,4,4]{0,2,1:T(4,128)S(1)} fusion(f32[4,256,128,4]{2,1,3,0:T(8,128)} %get-tuple-element.297, f32[128,4,4]{0,2,1:T(4,128)S(1)} %select_maximum_fusion.2, pred[128,256]{0,1:T(8,128)(4,1)S(1)} %compare_and_fusion.4), kind=kLoop, calls=%fused_computation.9.clone.1 | loop fusion | flops 2619392 | bytes 2146304 | tf_op jit(solution)/shard_map/while/body/eval_jaxpr/reduce_sum | solution.py:195
  123.4 3.5 %fusion.66 = f32[128,4,4,128]{0,3,2,1:T(8,128)} fusion(bf16[256,4,128,1]{0,2,3,1:T(8,128)(2,1)S(1)} %bitcast.105, f32[4,256,128,4]{2,1,3,0:T(8,128)} %get-tuple-element.297, f32[128,4,4,128]{0,3,2,1:T(8,128)} %get-tuple-element.319, f32[128,4,4]{0,2,1:T(4,128)S(1)} %select_maximum_fusion.2, pred[128,256]{0,1:T(8,128)(4,1)S(1)} %compare_and_fusion.4, ...), kind=kOutput, calls=%fused_computation.11.clone.1 | convolution fusion | flops 137625600 | bytes 4505601 | tf_op jit(solution)/shard_map/while/body/eval_jaxpr/qgjk,kgd->qgjd/dot_general | solution.py:196
  127.0 1.8 %all-gather.1 = f32[256,4,4]{0,2,1:T(4,128)S(1)} all-gather(f32[128,4,4]{0,2,1:T(4,128)S(1)} %get-tuple-element.87), channel_id=3, replica_groups=mesh['slot'=32,'row'=2,'col'=2] {'row'}, dimensions={0}, use_global_device_ids=true | all-gather | bytes 24576 | tf_op jit(solution)/shard_map/all_gather | solution.py:16
  128.8 1.8 %all-gather.2 = f32[256,4,4]{0,2,1:T(4,128)S(1)} all-gather(f32[128,4,4]{0,2,1:T(4,128)S(1)} %get-tuple-element.88), channel_id=4, replica_groups=mesh['slot'=32,'row'=2,'col'=2] {'row'}, dimensions={0}, use_global_device_ids=true | all-gather | bytes 24576 | tf_op jit(solution)/shard_map/all_gather | solution.py:16
  130.7 5.3 %all-gather.5.cloned.1.call-done = f32[256,4,4,128]{0,3,2,1:T(8,128)} async-done(((f32[128,4,4,128]{0,3,2,1:T(8,128)}), f32[256,4,4,128]{0,3,2,1:T(8,128)}) %all-gather.5.cloned.1.call-update) | async-done | bytes 2097168 | tf_op jit(solution)/shard_map/all_gather | solution.py:16
  136.0 1.8 %fusion.26 = bf16[128,4,4,128]{0,3,2,1:T(8,128)(2,1)S(1)} fusion(f32[256,4,4,128]{0,3,2,1:T(8,128)} %all-gather.5.cloned.1.call-done, f32[128,4,4]{0,2,1:T(4,128)S(1)} %get-tuple-element.195, f32[128,4,4]{0,2,1:T(4,128)S(1)} %get-tuple-element.197, f32[128,4,4]{0,2,1:T(4,128)S(1)} %get-tuple-element.196), kind=kLoop, calls=%fused_computation.50 | loop fusion | flops 1310720 | bytes 2646016 | tf_op jit(solution)/shard_map/convert_element_type | solution.py:214
  137.8 5.5 %convolution_convert_fusion = bf16[128,2048]{1,0:T(8,128)(2,1)} fusion(bf16[128,2048]{0,1:T(8,128)(2,1)S(1)} %bitcast.106, bf16[2048,2048]{1,0:T(8,128)(2,1)} %param.18), kind=kOutput, calls=%fused_computation.37 | convolution fusion | flops 1074003968 | bytes 9437184 | tf_op jit(solution)/shard_map/dot_general | solution.py:218
  143.2 18.1 %reduce-scatter.5.cloned.1.call-done = bf16[64,2048]{1,0:T(8,128)(2,1)} async-done(((bf16[128,2048]{1,0:T(8,128)(2,1)}), bf16[64,2048]{1,0:T(8,128)(2,1)}) %reduce-scatter.5.cloned.1.call-update) | async-done | bytes 262160 | tf_op jit(solution)/shard_map/reduce_scatter | solution.py:217
  (98 shorter events, 9.5 us)
Async XLA Ops:
  6.5 2.9 %copy-start = (bf16[128,2,8,512]{3,2,1,0:T(8,128)(2,1)S(1)}, bf16[128,2,8,512]{3,2,1,0:T(8,128)(2,1)}, u32[]{:S(2)}) copy-start(bf16[128,2,8,512]{3,2,1,0:T(8,128)(2,1)} %param.19) | copy-start | bytes 6291460
  14.4 12.8 %copy-start.5 = (bf16[1,128,2048]{2,1,0:T(8,128)(2,1)S(1)}, bf16[1,128,2048]{2,1,0:T(8,128)(2,1)}, u32[]{:S(2)}) copy-start(bf16[1,128,2048]{2,1,0:T(8,128)(2,1)} %param.14) | copy-start | bytes 1572868
  14.4 43.8 %all-to-all-start = ((bf16[64,2,2,8,512]{4,3,2,1,0:T(8,128)(2,1)}), bf16[64,2,2,8,512]{4,3,2,1,0:T(8,128)(2,1)}, u32[]{:S(2)}, u32[]{:S(2)}) async-start(bf16[64,2,2,8,512]{4,3,2,1,0:T(8,128)(2,1)} %bitcast.104), calls=%async_computation | async-start | bytes 4194304 | tf_op jit(solution)/shard_map/all_to_all | solution.py:100
  27.2 40.0 %reduce-scatter.7.cloned.1.call-start = ((), (), s32[]{:S(2)}) async-start(), calls=%async_computation.5 | async-start | bytes 2359296
  35.5 4.0 %copy-start.4 = (s32[32]{0:T(128)S(1)}, s32[32]{0:T(128)}, u32[]{:S(2)}) copy-start(s32[32]{0:T(128)} %param.22) | copy-start | bytes 388
  35.5 4.6 %copy-start.1 = (s32[8192]{0:T(1024)S(1)}, s32[8192]{0:T(1024)}, u32[]{:S(2)}) copy-start(s32[8192]{0:T(1024)} %param.20) | copy-start | bytes 98308
  35.5 7.2 %copy-start.3 = (s32[1,128]{1,0:T(1,128)S(1)}, s32[1,128]{1,0:T(1,128)}, u32[]{:S(2)}) copy-start(s32[1,128]{1,0:T(1,128)} %param.23) | copy-start | bytes 1540
  38.7 97.3 %all-gather.5.cloned.1.call-start = ((), (), s32[]{:S(2)}) async-start(), calls=%async_computation.4 | async-start | bytes 3145728 | tf_op jit(solution)/shard_map/all_gather | solution.py:16
  67.2 6.3 %copy-start.2 = (f32[64,3072]{1,0:T(8,128)S(1)}, f32[64,3072]{1,0:T(8,128)}, u32[]{:S(2)}) copy-start(f32[64,3072]{1,0:T(8,128)} %reduce-scatter.7.cloned.1.call-done) | copy-start | bytes 2359300
  127.0 34.4 %reduce-scatter.5.cloned.1.call-start = ((), (), s32[]{:S(2)}) async-start(), calls=%async_computation.3 | async-start | bytes 786432 | tf_op jit(solution)/shard_map/reduce_scatter | solution.py:217
Sparse Core Ops, SparseCore 0:
  38.8 13.2 reduce-scatter.6
  127.1 8.8 all-gather.4
  143.4 17.9 reduce-scatter.4
where the time goes:
time: 169 us; the launch traced here: 168 us
  waiting for transfers between devices  37.4 us (22%)
  matrix products  34.9 us (21%)
  local copies, waits for them, and re-layouts  32.8 us (19%)
  other arithmetic  23.2 us (14%)
  between operations  14.1 us (8%)
  starting transfers between devices  12.9 us (8%)
  blocking collectives  9.68 us (6%)
  loops' own time  2.93 us (2%)
    reduce_scatter x1, waiting for transfers between devices, on_device(): lax.psum_scatter(jnp.dot(row_block, w_out, preferred_element_type=jnp.flo...  18.1 us
    all_to_all x1, waiting for transfers between devices, on_device(): lax.all_to_all(outgoing, ('slot', 'row'), split_axis=0, concat_axis=0, ti...  13.9 us
    dot_general x4, matrix products, attend(): jnp.einsum('qgjk,kgd->qgjd', probs.astype(jnp.bfloat16), value_block, pre...  13.7 us
    all_to_all x1, starting transfers between devices, on_device(): lax.all_to_all(outgoing, ('slot', 'row'), split_axis=0, concat_axis=0, ti...  12.8 us
    reduce_sum x4, other arithmetic, attend(): weight_sum = weight_sum * factor + jnp.sum(probs, axis=3)  8.4 us
    dot_general x1, matrix products, on_device(): jnp.dot(row_block, weights, preferred_element_type=jnp.float32)  8.3 us
    dot_general x4, matrix products, attend(): jnp.einsum('qgjd,kgd->qgjk', grouped, key_block, preferred_element_type=j...  7.42 us
    dot_general x1, matrix products, on_device(): jnp.dot(row_block, w_out, preferred_element_type=jnp.float32)  5.46 us
  transfers between devices with their start and end apart: 4, of which 3 were waited for; matrix products, arithmetic and copies ran while one was open for 15% of the time, Pallas kernels for 0%

commit v1 on v0

v1 whole, which is shorter than its diff:
```python
import functools
import math

import jax
import jax.numpy as jnp
import numpy as np
from jax import lax
from jax.experimental import pallas as pl
from jax.experimental.pallas import tpu as pltpu
from jax.sharding import PartitionSpec as P

HEAD = 128
ROPE_BASE = 500000.0
NEG = -1e30
FAR = 1 << 20
MESH = pl.DeviceIdType.MESH
SCALE = math.log2(math.e) / math.sqrt(HEAD)
f32, bf16, i32 = jnp.float32, jnp.bfloat16, jnp.int32

TOK = 128
NZ, NY, NX = 4, 4, 2
STEPS = NZ * NY * NX
CHUNK = 4
CHUNKS = STEPS // CHUNK
MSG = 32
KEYS = CHUNK * 2 * MSG


def offsets(inner, outer):
    b, c = outer % 4, outer // 4
    return inner, (inner + b) % 4, (inner + b + c) % 2


def kernel(
    hidden, w_query, key_weight, value_weight, w_out, kv_store,
    offset_in, tiles_in, count, pos_in, freq_in,
    out,
    hid, wq, wk, wv, wo, kv, offs, tiles, pos_v, freq_v,
    send, recv, ids_v, ids, turn_c, turn_s,
    part_send, part_recv, part_own,
    q, k_new, v_new, owner_sel, pos_m,
    m_s, l_s, acc, att, o_acc, o_send, o_recv,
    load_sem, small_sem, ids_sem, w_sem, self_sem, send_sem, recv_sem,
    pair_send, pair_recv, part_ssem, part_rsem, att_ssem, att_rsem, o_ssem, o_rsem,
):
    s = lax.axis_index("slot")
    r = lax.axis_index("row")
    c = lax.axis_index("col")
    z, y, x = s // (NY * NX), (s // NX) % NY, s % NX
    me = s * 2 + r
    sign = 1 - 2 * r

    def target(step):
        dz, dy, dx = offsets(step % 4, step // 4)
        return ((z + sign * dz + 4) % 4 * NY + (y + sign * dy + 4) % 4) * NX + (x + dx) % 2

    barrier = pltpu.get_barrier_semaphore()
    pl.semaphore_signal(barrier, 1, device_id={"row": 1 - r}, device_id_type=MESH)
    pl.semaphore_signal(barrier, 1, device_id={"col": 1 - c}, device_id_type=MESH)

    def greet(slot, carry):
        @pl.when(slot != s)
        def _():
            pl.semaphore_signal(barrier, 1, device_id={"slot": slot, "row": 0}, device_id_type=MESH)
            pl.semaphore_signal(barrier, 1, device_id={"slot": slot, "row": 1}, device_id_type=MESH)

        return carry

    loads = [
        pltpu.make_async_copy(tiles_in.at[:, pl.ds(0, HEAD)], tiles.at[0], small_sem.at[0]),
        pltpu.make_async_copy(tiles_in.at[:, pl.ds(HEAD, HEAD)], tiles.at[1], small_sem.at[4]),
        pltpu.make_async_copy(offset_in, offs, small_sem.at[1]),
        pltpu.make_async_copy(pos_in, pos_v, small_sem.at[2]),
        pltpu.make_async_copy(freq_in, freq_v, small_sem.at[3]),
    ]
    kv_load = pltpu.make_async_copy(kv_store, kv, load_sem.at[0])
    hid_load = pltpu.make_async_copy(hidden.at[0], hid, load_sem.at[1])
    w_loads = [
        pltpu.make_async_copy(a, b, w_sem.at[n])
        for n, (a, b) in enumerate(((w_query, wq), (key_weight, wk), (value_weight, wv), (w_out, wo)))
    ]
    for copy in loads + [kv_load, hid_load] + w_loads:
        copy.start()
    lax.fori_loop(0, STEPS, greet, 0)
    for copy in loads:
        copy.wait()

    lane = lax.broadcasted_iota(i32, (STEPS, HEAD), 1)
    mine_offs = offs[pl.ds(me, 1), :]
    freq = freq_v[...]
    half_sign = jnp.where(lax.broadcasted_iota(i32, (1, HEAD), 1) < HEAD // 2, -1.0, 1.0)
    id_rows = jnp.zeros((STEPS, HEAD), i32)
    for b in range(2):
        block = tiles[b]
        mine = (block >> 7) == me
        code = lane * HEAD + (block & 127)
        picks = (
            jnp.min(jnp.where(mine, code, FAR), axis=1, keepdims=True),
            jnp.max(jnp.where(mine, code, 0), axis=1, keepdims=True),
        )
        for k, pick in enumerate(picks):
            local, tile = pick & 127, pick >> 7
            offset = jnp.sum(jnp.where(lane == local, mine_offs, 0), axis=1, keepdims=True)
            angle = ((b * HEAD + tile) * 8 - offset).astype(f32) * freq
            turn_c[b * 2 + k] = jnp.cos(angle)
            turn_s[b * 2 + k] = jnp.sin(angle) * half_sign
            id_rows = jnp.where(lane == b * 2 + k, local, id_rows)
    ids_v[...] = id_rows
    id_copy = pltpu.make_async_copy(ids_v, ids, ids_sem)
    id_copy.start()
    id_copy.wait()
    kv_load.wait()

    def pack(step, slot):
        for b in range(2):
            for kind in range(2):
                rows = []
                for k in range(2):
                    rows.append(kv[ids[slot, b * 2 + k], kind].astype(f32))
                for h in range(4):
                    heads = []
                    for k in range(2):
                        u = rows[k][:, h * HEAD : (h + 1) * HEAD]
                        if kind == 0:
                            cosine = turn_c[b * 2 + k, pl.ds(slot, 1), :]
                            sine = turn_s[b * 2 + k, pl.ds(slot, 1), :]
                            u = u * cosine + pltpu.roll(u, HEAD // 2, axis=1) * sine
                        heads.append(u)
                    send[step * 2 + h // 2, kind, b * 16 : (b + 1) * 16, (h % 2) * HEAD : (h % 2 + 1) * HEAD] = (
                        jnp.concatenate(heads, axis=0).astype(bf16)
                    )

    pl.semaphore_wait(barrier, 2 * STEPS)

    pack(0, s)
    self_copy = pltpu.make_async_copy(send.at[r], recv.at[r], self_sem)
    self_copy.start()
    pair_copy = pltpu.make_async_remote_copy(
        send.at[1 - r], recv.at[r], pair_send, pair_recv, device_id={"row": 1 - r}, device_id_type=MESH
    )
    pair_copy.start()

    def ship(step, carry):
        slot = target(step)
        pack(step, slot)
        for row in range(2):
            pltpu.make_async_remote_copy(
                send.at[step * 2 + row],
                recv.at[step * 2 + r],
                send_sem,
                recv_sem.at[step // CHUNK],
                device_id={"slot": slot, "row": row},
                device_id_type=MESH,
            ).start()
        return carry

    lax.fori_loop(1, STEPS, ship, 0)

    hid_load.wait()
    for copy in w_loads[:3]:
        copy.wait()
    x_in = hid[...]

    def project(side, into):
        def body(n, carry):
            cols = pl.ds(pl.multiple_of(side * 1024 + n * 256, 256), 256)
            into[:, pl.ds(pl.multiple_of(n * 256, 256), 256)] = jnp.dot(
                x_in, wq[:, cols], preferred_element_type=f32
            )
            return carry

        lax.fori_loop(0, 4, body, 0)
        cols = pl.ds(pl.multiple_of(side * 256, 256), 256)
        into[:, 1024:1280] = jnp.dot(x_in, wk[:, cols], preferred_element_type=f32)
        into[:, 1280:1536] = jnp.dot(x_in, wv[:, cols], preferred_element_type=f32)

    project(1 - r, part_send)
    part_copy = pltpu.make_async_remote_copy(
        part_send, part_recv, part_ssem, part_rsem, device_id={"row": 1 - r}, device_id_type=MESH
    )
    part_copy.start()
    project(r, part_own)

    def column(row_vector):
        return jnp.transpose(jnp.broadcast_to(row_vector, (HEAD, HEAD)))

    pos_col = column(pos_v[...])
    pos_m[:, :HEAD] = pos_col
    pos_m[:, HEAD:] = pos_col
    owner_cols = [column(tiles[b, pl.ds(s, 1), :] >> 7) for b in range(2)]
    block_of = (lax.broadcasted_iota(i32, (TOK, HEAD), 1) >> 4) & 1
    picked = jnp.where(block_of == 0, owner_cols[0], owner_cols[1])
    owner_sel[:, :HEAD] = picked
    owner_sel[:, HEAD:] = picked
    token_angle = pos_col.astype(f32) * freq
    token_c = jnp.cos(token_angle)
    token_s = jnp.sin(token_angle) * half_sign

    part_copy.wait()

    def total(lo):
        return part_own[:, lo : lo + HEAD] + part_recv[:, lo : lo + HEAD]

    def turned(lo):
        u = total(lo)
        return (u * token_c + pltpu.roll(u, HEAD // 2, axis=1) * token_s).astype(bf16)

    for h in range(8):
        q[h] = turned(h * HEAD)
    for h in range(2):
        k_new[:, h * HEAD : (h + 1) * HEAD] = turned(1024 + h * HEAD)
        v_new[:, h * HEAD : (h + 1) * HEAD] = total(1280 + h * HEAD).astype(bf16)

    def scores(qh, kh, mask):
        sc = lax.dot_general(qh, kh, (((1,), (1,)), ((), ())), preferred_element_type=f32)
        return jnp.where(mask, sc * SCALE, NEG)

    fresh = lax.broadcasted_iota(i32, (TOK, TOK), 1) <= lax.broadcasted_iota(i32, (TOK, TOK), 0)
    for h in range(8):
        g = h // 4
        sc = scores(q[h], k_new[:, g * HEAD : (g + 1) * HEAD], fresh)
        peak = jnp.max(sc, axis=1, keepdims=True)
        p = jnp.exp2(sc - peak)
        m_s[h] = jnp.broadcast_to(peak, (TOK, HEAD))
        l_s[h] = jnp.broadcast_to(jnp.sum(p, axis=1, keepdims=True), (TOK, HEAD))
        acc[h] = jnp.dot(p.astype(bf16), v_new[:, g * HEAD : (g + 1) * HEAD], preferred_element_type=f32)

    limit = count[s] * 8
    lane2 = lax.broadcasted_iota(i32, (1, KEYS), 1)
    src = lane2 >> 5
    in_block, second, unit = (lane2 >> 4) & 1, (lane2 >> 3) & 1, lane2 & 7
    src_row = src & 1
    src_sign = 1 - 2 * src_row
    tile_row = lax.broadcasted_iota(i32, (TOK, KEYS), 0)

    def attend(n, carry):
        inner = src >> 1
        b, cc = n % 4, n // 4
        dz, dy, dx = inner, (inner + b) & 3, (inner + b + cc) & 1
        source = ((((z - src_sign * dz + 4) & 3) * NY + ((y - src_sign * dy + 4) & 3)) * NX + ((x + dx) & 1)) * 2 + src_row
        here = owner_sel[...] == source
        first = jnp.min(jnp.where(here, tile_row, FAR), axis=0, keepdims=True)
        last = jnp.max(jnp.where(here, tile_row, 0), axis=0, keepdims=True)
        key_pos = (in_block * HEAD + jnp.where(second == 0, first, last)) * 8 + unit
        pos = pos_m[...]
        redone = jnp.max(jnp.where(pos == key_pos, 1, 0), axis=0, keepdims=True)
        key_pos = jnp.where(jnp.logical_or(redone > 0, key_pos >= limit), FAR, key_pos)
        mask = key_pos <= pos
        for g in range(2):
            kh = recv[pl.ds(n * 8, 8), 0, :, g * HEAD : (g + 1) * HEAD].reshape(KEYS, HEAD)
            vh = recv[pl.ds(n * 8, 8), 1, :, g * HEAD : (g + 1) * HEAD].reshape(KEYS, HEAD)
            for j in range(4):
                h = g * 4 + j
                sc = scores(q[h], kh, mask)
                old = m_s[h]
                peak = jnp.maximum(old, jnp.max(sc, axis=1, keepdims=True))
                p = jnp.exp2(sc - jnp.concatenate([peak, peak], axis=1))
                shrink = jnp.exp2(old - peak)
                m_s[h] = peak
                l_s[h] = l_s[h] * shrink + jnp.sum(p, axis=1, keepdims=True)
                acc[h] = acc[h] * shrink + jnp.dot(p.astype(bf16), vh, preferred_element_type=f32)
        return carry

    def landed(first, many, sem):
        return pltpu.make_async_copy(
            recv.at[pl.ds(first, many)], recv.at[pl.ds(first, many)], sem
        )

    self_copy.wait()
    pair_copy.wait()
    for n in range(CHUNKS):
        if n == 0:
            landed(2, 6, recv_sem.at[0]).wait()
        else:
            landed(8 * n, 8, recv_sem.at[n]).wait()
        attend(n, 0)

    for h in range(8):
        att[r, :, h * HEAD : (h + 1) * HEAD] = (acc[h] / l_s[h]).astype(bf16)
    att_copy = pltpu.make_async_remote_copy(
        att.at[r], att.at[r], att_ssem, att_rsem, device_id={"row": 1 - r}, device_id_type=MESH
    )
    att_copy.start()
    w_loads[3].wait()

    def out_cols(n):
        return pl.ds(pl.multiple_of(n * 256, 256), 256)

    def first_half(n, carry):
        rows = pl.ds(pl.multiple_of(r * 1024, 1024), 1024)
        o_acc[:, out_cols(n)] = jnp.dot(att[r], wo[rows, out_cols(n)], preferred_element_type=f32)
        return carry

    lax.fori_loop(0, 8, first_half, 0)
    att_copy.wait()

    def o_copy(n):
        return pltpu.make_async_remote_copy(
            o_send.at[n], o_recv.at[n], o_ssem.at[n], o_rsem.at[n], device_id={"col": 1 - c}, device_id_type=MESH
        )

    def second_half(n, carry):
        rows = pl.ds(pl.multiple_of((1 - r) * 1024, 1024), 1024)
        o_acc[:, out_cols(n)] += jnp.dot(att[1 - r], wo[rows, out_cols(n)], preferred_element_type=f32)
        o_send[n] = o_acc[pl.ds(pl.multiple_of((1 - c) * 64, 64), 64), out_cols(n)].astype(bf16)
        o_copy(n).start()
        return carry

    lax.fori_loop(0, 8, second_half, 0)
    own_rows = pl.ds(pl.multiple_of(c * 64, 64), 64)

    def finish(n, carry):
        o_copy(n).wait()
        out[0, :, out_cols(n)] = (o_acc[own_rows, out_cols(n)] + o_recv[n].astype(f32)).astype(bf16)
        return carry

    lax.fori_loop(0, 8, finish, 0)
    pltpu.make_async_copy(send.at[pl.ds(2, 62)], send.at[pl.ds(2, 62)], send_sem).wait()


def on_device(
    hidden, w_query, key_weight, value_weight, w_out, kv_store,
    stretch_offset, tile_stretch, slot_count, recomp_pos,
):
    freq = (ROPE_BASE ** (-2.0 * np.arange(HEAD // 2, dtype=np.float32) / HEAD)).astype(np.float32)
    freq = jnp.asarray(np.concatenate([freq, freq])[None, :])
    anywhere = pl.BlockSpec(memory_space=pl.ANY)
    dma = pltpu.SemaphoreType.DMA
    return pl.pallas_call(
        kernel,
        out_shape=jax.ShapeDtypeStruct((1, 64, 2048), bf16),
        in_specs=[anywhere] * 8 + [pl.BlockSpec(memory_space=pltpu.SMEM)] + [anywhere] * 2,
        out_specs=pl.BlockSpec(memory_space=pltpu.VMEM),
        scratch_shapes=[
            pltpu.VMEM((TOK, 2048), bf16),
            pltpu.VMEM((2048, 2048), bf16),
            pltpu.VMEM((2048, 512), bf16),
            pltpu.VMEM((2048, 512), bf16),
            pltpu.VMEM((2048, 2048), bf16),
            pltpu.VMEM((128, 2, 8, 512), bf16),
            pltpu.VMEM((64, 128), i32),
            pltpu.VMEM((2, 32, 128), i32),
            pltpu.VMEM((1, 128), i32),
            pltpu.VMEM((1, 128), f32),
            pltpu.VMEM((2 * STEPS, 2, MSG, 256), bf16),
            pltpu.VMEM((2 * STEPS, 2, MSG, 256), bf16),
            pltpu.VMEM((STEPS, HEAD), i32),
            pltpu.SMEM((STEPS, HEAD), i32),
            pltpu.VMEM((4, STEPS, HEAD), f32),
            pltpu.VMEM((4, STEPS, HEAD), f32),
            pltpu.VMEM((TOK, 1536), f32),
            pltpu.VMEM((TOK, 1536), f32),
            pltpu.VMEM((TOK, 1536), f32),
            pltpu.VMEM((8, TOK, HEAD), bf16),
            pltpu.VMEM((TOK, 256), bf16),
            pltpu.VMEM((TOK, 256), bf16),
            pltpu.VMEM((TOK, KEYS), i32),
            pltpu.VMEM((TOK, KEYS), i32),
            pltpu.VMEM((8, TOK, HEAD), f32),
            pltpu.VMEM((8, TOK, HEAD), f32),
            pltpu.VMEM((8, TOK, HEAD), f32),
            pltpu.VMEM((2, TOK, 1024), bf16),
            pltpu.VMEM((TOK, 2048), f32),
            pltpu.VMEM((8, 64, 256), bf16),
            pltpu.VMEM((8, 64, 256), bf16),
            dma((2,)), dma((5,)), dma(()), dma((4,)), dma(()), dma(()), dma((CHUNKS,)),
            dma(()), dma(()), dma(()), dma(()), dma(()), dma(()), dma((8,)), dma((8,)),
        ],
        compiler_params=pltpu.CompilerParams(
            collective_id=0, has_side_effects=True, vmem_limit_bytes=58 << 20
        ),
        name="joined_attention",
    )(
        hidden, w_query, key_weight, value_weight, w_out, kv_store,
        stretch_offset.reshape(64, 128), tile_stretch, slot_count, recomp_pos, freq,
    )


def solution(mesh):
    return jax.shard_map(
        on_device,
        mesh=mesh,
        in_specs=(
            P("slot", None, "row"),
            P("row", "col"),
            P("row", "col"),
            P("row", "col"),
            P("col", "row"),
            P(("slot", "row"), None, None, "col"),
            P(),
            P(),
            P(),
            P("slot", None),
        ),
        out_specs=P("slot", "col", "row"),
        check_vma=False,
    )
```

time: 169 us -> 52.9 us (0.31)
  Pallas kernels: 0 us -> 51.1 us
  waiting for transfers between devices: 37.4 us -> 0 us
  matrix products: 34.9 us -> 0 us
  local copies, waits for them, and re-layouts: 32.8 us -> 1.67 us
  other arithmetic: 23.2 us -> 0 us
  between operations: 14.1 us -> 0.01 us
  starting transfers between devices: 12.9 us -> 0 us
  blocking collectives: 9.68 us -> 0 us
  loops' own time: 2.93 us -> 0 us
    pallas_call x0 -> x1, Pallas kernels: none -> 51.1 us  [on_device(): pl.pallas_call(kernel, out_shape=jax.ShapeDtypeStruct((1, 64, 2048), bf16...]
    dot_general x10 -> x0, matrix products: 34.9 us -> none  [the longest x4 13.7 us: attend(): jnp.einsum('qgjk,kgd->qgjd', probs.astype(jnp.bfloat16), value_block, pre...]
    reduce_scatter x1 -> x0, waiting for transfers between devices: 18.1 us -> none  [on_device(): lax.psum_scatter(jnp.dot(row_block, w_out, preferred_element_type=jnp.flo...]
    all_to_all x1 -> x0, waiting for transfers between devices: 13.9 us -> none  [on_device(): lax.all_to_all(outgoing, ('slot', 'row'), split_axis=0, concat_axis=0, ti...]
    all_to_all x1 -> x0, starting transfers between devices: 12.8 us -> none  [on_device(): lax.all_to_all(outgoing, ('slot', 'row'), split_axis=0, concat_axis=0, ti...]
    all_gather x5 -> x0, blocking collectives: 9.68 us -> none  [the longest x2 3.63 us: joined(): pieces = jax.tree.map(lambda part: lax.all_gather(part, axis), value)]
    reduce_sum x6 -> x0, other arithmetic: 8.72 us -> none  [the longest x4 8.4 us: attend(): weight_sum = weight_sum * factor + jnp.sum(probs, axis=3)]
    dynamic_slice x17 -> x0, local copies, waits for them, and re-layouts: 8.59 us -> none  [the longest x8 4.81 us: attend(): lax.dynamic_slice_in_dim(joined_values, span_start, key_span, 0)]
  transfers between devices with their start and end apart: 4 -> 0, of which waited for: 3 -> 0; matrix products, arithmetic and copies ran while one was open for 15% -> 0% of each run, Pallas kernels for 0% -> 0%
where the time goes in v1:
time: 52.9 us; the launch traced here: 52.7 us
  Pallas kernels  51.1 us (97%)
  local copies, waits for them, and re-layouts  1.67 us (3%)
    pallas_call x1, Pallas kernels, on_device(): pl.pallas_call(kernel, out_shape=jax.ShapeDtypeStruct((1, 64, 2048), bf16...  51.1 us
    unnamed x1, local copies, waits for them, and re-layouts  1.67 us

profile of v1, /device:TPU:1, one launch (start us, length us, event | category | flops | bytes accessed | tf_op | source)
XLA Modules:
  0.0 52.7 jit_solution(8517141533877656149)
XLA Ops:
  0.0 51.1 %joined_attention.1 = bf16[1,64,2048]{2,1,0:T(8,128)(2,1)} custom-call(bf16[1,128,2048]{2,1,0:T(8,128)(2,1)} %hidden.1, bf16[2048,2048]{1,0:T(8,128)(2,1)} %w_query.1, bf16[2048,512]{1,0:T(8,128)(2,1)} %key_weight.1, bf16[2048,512]{1,0:T(8,128)(2,1)} %value_weight.1, bf16[2048,2048]{1,0:T(8,128)(2,1)} %w_out.1, bf16[128,2,8,512]{3,2,1,0:T(8,128)(2,1)} %kv_store.1, ...), custom_call_target="tpu_custom_call" | custom-call | tf_op jit(solution)/shard_map/joined_attention/pallas_call | solution.py:329
  51.1 1.7 %copy.13 = bf16[1,64,2048]{2,1,0:T(8,128)(2,1)} copy(bf16[1,64,2048]{2,1,0:T(8,128)(2,1)} %joined_attention.1) | data formatting | bytes 524288

commit v2 on v1

--- a/solution.py
+++ b/solution.py
@@ -33,9 +33,9 @@
 
 def kernel(
     hidden, w_query, key_weight, value_weight, w_out, kv_store,
-    offset_in, tiles_in, count, pos_in, freq_in,
+    offset_in, tiles_in, count_in, pos_in, freq_in,
     out,
-    hid, wq, wk, wv, wo, kv, offs, tiles, pos_v, freq_v,
+    hid, wq, wk, wv, wo, kv, offs, tiles, count, pos_v, freq_v,
     send, recv, ids_v, ids, turn_c, turn_s,
     part_send, part_recv, part_own,
     q, k_new, v_new, owner_sel, pos_m,
@@ -71,6 +71,7 @@
         pltpu.make_async_copy(tiles_in.at[:, pl.ds(HEAD, HEAD)], tiles.at[1], small_sem.at[4]),
         pltpu.make_async_copy(offset_in, offs, small_sem.at[1]),
         pltpu.make_async_copy(pos_in, pos_v, small_sem.at[2]),
+        pltpu.make_async_copy(count_in, count, small_sem.at[5]),
         pltpu.make_async_copy(freq_in, freq_v, small_sem.at[3]),
     ]
     kv_load = pltpu.make_async_copy(kv_store, kv, load_sem.at[0])
@@ -79,7 +80,7 @@
         pltpu.make_async_copy(a, b, w_sem.at[n])
         for n, (a, b) in enumerate(((w_query, wq), (key_weight, wk), (value_weight, wv), (w_out, wo)))
     ]
-    for copy in loads + [kv_load, hid_load] + w_loads:
+    for copy in loads + [kv_load]:
         copy.start()
     lax.fori_loop(0, STEPS, greet, 0)
     for copy in loads:
@@ -110,6 +111,8 @@
     id_copy.start()
     id_copy.wait()
     kv_load.wait()
+    for copy in [hid_load] + w_loads:
+        copy.start()
 
     def pack(step, slot):
         for b in range(2):
@@ -233,7 +236,7 @@
     src_sign = 1 - 2 * src_row
     tile_row = lax.broadcasted_iota(i32, (TOK, KEYS), 0)
 
-    def attend(n, carry):
+    def attend(n, done=None):
         inner = src >> 1
         b, cc = n % 4, n // 4
         dz, dy, dx = inner, (inner + b) & 3, (inner + b + cc) & 1
@@ -259,12 +262,24 @@
                 m_s[h] = peak
                 l_s[h] = l_s[h] * shrink + jnp.sum(p, axis=1, keepdims=True)
                 acc[h] = acc[h] * shrink + jnp.dot(p.astype(bf16), vh, preferred_element_type=f32)
-        return carry
+                if done is not None:
+                    done(h)
 
     def landed(first, many, sem):
         return pltpu.make_async_copy(
             recv.at[pl.ds(first, many)], recv.at[pl.ds(first, many)], sem
         )
+
+    def att_copy(n):
+        part = att.at[r]
+        return pltpu.make_async_remote_copy(
+            part, part, att_ssem.at[n], att_rsem.at[n], device_id={"row": 1 - r}, device_id_type=MESH
+        )
+
+    def share(h):
+        att[r, :, h * HEAD : (h + 1) * HEAD] = (acc[h] / l_s[h]).astype(bf16)
+        if h == 7:
+            att_copy(0).start()
 
     self_copy.wait()
     pair_copy.wait()
@@ -273,14 +288,10 @@
             landed(2, 6, recv_sem.at[0]).wait()
         else:
             landed(8 * n, 8, recv_sem.at[n]).wait()
-        attend(n, 0)
+        attend(n)
 
     for h in range(8):
-        att[r, :, h * HEAD : (h + 1) * HEAD] = (acc[h] / l_s[h]).astype(bf16)
-    att_copy = pltpu.make_async_remote_copy(
-        att.at[r], att.at[r], att_ssem, att_rsem, device_id={"row": 1 - r}, device_id_type=MESH
-    )
-    att_copy.start()
+        share(h)
     w_loads[3].wait()
 
     def out_cols(n):
@@ -292,7 +303,7 @@
         return carry
 
     lax.fori_loop(0, 8, first_half, 0)
-    att_copy.wait()
+    att_copy(0).wait()
 
     def o_copy(n):
         return pltpu.make_async_remote_copy(
@@ -306,8 +317,8 @@
         o_copy(n).start()
         return carry
 
+    own_rows = pl.ds(pl.multiple_of(c * 64, 64), 64)
     lax.fori_loop(0, 8, second_half, 0)
-    own_rows = pl.ds(pl.multiple_of(c * 64, 64), 64)
 
     def finish(n, carry):
         o_copy(n).wait()
@@ -324,12 +335,15 @@
 ):
     freq = (ROPE_BASE ** (-2.0 * np.arange(HEAD // 2, dtype=np.float32) / HEAD)).astype(np.float32)
     freq = jnp.asarray(np.concatenate([freq, freq])[None, :])
-    anywhere = pl.BlockSpec(memory_space=pl.ANY)
     dma = pltpu.SemaphoreType.DMA
+    operands = (
+        hidden, w_query, key_weight, value_weight, w_out, kv_store,
+        stretch_offset.reshape(64, 128), tile_stretch, slot_count, recomp_pos, freq,
+    )
     return pl.pallas_call(
         kernel,
         out_shape=jax.ShapeDtypeStruct((1, 64, 2048), bf16),
-        in_specs=[anywhere] * 8 + [pl.BlockSpec(memory_space=pltpu.SMEM)] + [anywhere] * 2,
+        in_specs=[pl.BlockSpec(memory_space=pltpu.HBM)] * 11,
         out_specs=pl.BlockSpec(memory_space=pltpu.VMEM),
         scratch_shapes=[
             pltpu.VMEM((TOK, 2048), bf16),
@@ -340,6 +354,7 @@
             pltpu.VMEM((128, 2, 8, 512), bf16),
             pltpu.VMEM((64, 128), i32),
             pltpu.VMEM((2, 32, 128), i32),
+            pltpu.SMEM((32,), i32),
             pltpu.VMEM((1, 128), i32),
             pltpu.VMEM((1, 128), f32),
             pltpu.VMEM((2 * STEPS, 2, MSG, 256), bf16),
@@ -363,17 +378,14 @@
             pltpu.VMEM((TOK, 2048), f32),
             pltpu.VMEM((8, 64, 256), bf16),
             pltpu.VMEM((8, 64, 256), bf16),
-            dma((2,)), dma((5,)), dma(()), dma((4,)), dma(()), dma(()), dma((CHUNKS,)),
-            dma(()), dma(()), dma(()), dma(()), dma(()), dma(()), dma((8,)), dma((8,)),
+            dma((2,)), dma((6,)), dma(()), dma((4,)), dma(()), dma(()), dma((CHUNKS,)),
+            dma(()), dma(()), dma(()), dma(()), dma((4,)), dma((4,)), dma((8,)), dma((8,)),
         ],
         compiler_params=pltpu.CompilerParams(
-            collective_id=0, has_side_effects=True, vmem_limit_bytes=58 << 20
+            collective_id=0, has_side_effects=True, vmem_limit_bytes=44 << 20
         ),
         name="joined_attention",
-    )(
-        hidden, w_query, key_weight, value_weight, w_out, kv_store,
-        stretch_offset.reshape(64, 128), tile_stretch, slot_count, recomp_pos, freq,
-    )
+    )(*(pltpu.with_memory_space_constraint(a, pltpu.HBM) for a in operands))
 
 
 def solution(mesh):

time: 52.9 us -> 48.6 us (0.919)
  Pallas kernels: 51.1 us -> 47.8 us
  local copies, waits for them, and re-layouts: 1.67 us -> 0.71 us
    pallas_call x1, Pallas kernels: 51.1 us -> 47.8 us  [on_device(): pl.pallas_call(kernel, out_shape=jax.ShapeDtypeStruct((1, 64, 2048), bf16...]
    unnamed x1, local copies, waits for them, and re-layouts: 1.67 us -> 0.71 us
where the time goes in v2:
time: 48.6 us; the launch traced here: 48.5 us
  Pallas kernels  47.8 us (98%)
  local copies, waits for them, and re-layouts  0.71 us (1%)
    pallas_call x1, Pallas kernels, on_device(): pl.pallas_call(kernel, out_shape=jax.ShapeDtypeStruct((1, 64, 2048), bf16...  47.8 us

profile of v2, /device:TPU:1, one launch (start us, length us, event | category | flops | bytes accessed | tf_op | source)
XLA Modules:
  0.0 48.5 jit_solution(15598095567050650789)
XLA Ops:
  0.0 47.8 %joined_attention.1 = bf16[1,64,2048]{2,1,0:T(8,128)(2,1)S(1)} custom-call(bf16[1,128,2048]{2,1,0:T(8,128)(2,1)} %hidden.1, bf16[2048,2048]{1,0:T(8,128)(2,1)} %w_query.1, bf16[2048,512]{1,0:T(8,128)(2,1)} %key_weight.1, bf16[2048,512]{1,0:T(8,128)(2,1)} %value_weight.1, bf16[2048,2048]{1,0:T(8,128)(2,1)} %w_out.1, bf16[128,2,8,512]{3,2,1,0:T(8,128)(2,1)} %kv_store.1, ...), custom_call_target="tpu_custom_call" | custom-call | tf_op jit(solution)/shard_map/joined_attention/pallas_call | solution.py:343
  47.8 0.7 %copy.13 = bf16[1,64,2048]{2,1,0:T(8,128)(2,1)} copy(bf16[1,64,2048]{2,1,0:T(8,128)(2,1)S(1)} %joined_attention.1) | data formatting | bytes 524288

commit v3 on v2

--- a/solution.py
+++ b/solution.py
@@ -26,22 +26,29 @@
 KEYS = CHUNK * 2 * MSG
 
 
-def offsets(inner, outer):
-    b, c = outer % 4, outer // 4
-    return inner, (inner + b) % 4, (inner + b + c) % 2
+def send_order():
+    order = [(0, 0, 0)]
+    for j in range(1, 4):
+        order += [(j, 0, 0), (0, j, 0)]
+    order += [(0, 0, 1)]
+    for j in range(1, 4):
+        order += [(j, 0, 1), (0, j, 1)] + [(j, 1 + (j + n) % 3, 0) for n in range(3)]
+    for m in range(9):
+        order += [(1 + m // 3, 1 + (m // 3 + m) % 3, 1)]
+    return order
 
 
 def kernel(
     hidden, w_query, key_weight, value_weight, w_out, kv_store,
-    offset_in, tiles_in, count_in, pos_in, freq_in,
+    offset_in, tiles_in, count_in, pos_in, freq_in, steps_in,
     out,
-    hid, wq, wk, wv, wo, kv, offs, tiles, count, pos_v, freq_v,
+    hid, wq, wk, wv, wo, kv, offs, tiles, count, pos_v, freq_v, steps_v,
     send, recv, ids_v, ids, turn_c, turn_s,
     part_send, part_recv, part_own,
     q, k_new, v_new, owner_sel, pos_m,
     m_s, l_s, acc, att, o_acc, o_send, o_recv,
     load_sem, small_sem, ids_sem, w_sem, self_sem, send_sem, recv_sem,
-    pair_send, pair_recv, part_ssem, part_rsem, att_ssem, att_rsem, o_ssem, o_rsem,
+    pair_send, pair_recv, part_ssem, part_rsem, att_ssem, att_rsem, o_ssem, o_rsem, second_stage, third_stage,
 ):
     s = lax.axis_index("slot")
     r = lax.axis_index("row")
@@ -50,21 +57,21 @@
     me = s * 2 + r
     sign = 1 - 2 * r
 
-    def target(step):
-        dz, dy, dx = offsets(step % 4, step // 4)
+    def target(dz, dy, dx):
         return ((z + sign * dz + 4) % 4 * NY + (y + sign * dy + 4) % 4) * NX + (x + dx) % 2
+
+    near = [target(j, 0, 0) for j in range(1, 4)] + [target(0, j, 0) for j in range(1, 4)] + [target(0, 0, 1)]
 
     barrier = pltpu.get_barrier_semaphore()
     pl.semaphore_signal(barrier, 1, device_id={"row": 1 - r}, device_id_type=MESH)
     pl.semaphore_signal(barrier, 1, device_id={"col": 1 - c}, device_id_type=MESH)
-
-    def greet(slot, carry):
-        @pl.when(slot != s)
-        def _():
-            pl.semaphore_signal(barrier, 1, device_id={"slot": slot, "row": 0}, device_id_type=MESH)
-            pl.semaphore_signal(barrier, 1, device_id={"slot": slot, "row": 1}, device_id_type=MESH)
-
-        return carry
+    for slot in near:
+        for row in range(2):
+            pl.semaphore_signal(barrier, 1, device_id={"slot": slot, "row": row}, device_id_type=MESH)
+
+    def tell(stage):
+        for slot in near:
+            pl.semaphore_signal(stage, 1, device_id={"slot": slot}, device_id_type=MESH)
 
     loads = [
         pltpu.make_async_copy(tiles_in.at[:, pl.ds(0, HEAD)], tiles.at[0], small_sem.at[0]),
@@ -72,6 +79,7 @@
         pltpu.make_async_copy(offset_in, offs, small_sem.at[1]),
         pltpu.make_async_copy(pos_in, pos_v, small_sem.at[2]),
         pltpu.make_async_copy(count_in, count, small_sem.at[5]),
+        pltpu.make_async_copy(steps_in, steps_v, small_sem.at[6]),
         pltpu.make_async_copy(freq_in, freq_v, small_sem.at[3]),
     ]
     kv_load = pltpu.make_async_copy(kv_store, kv, load_sem.at[0])
@@ -82,7 +90,6 @@
     ]
     for copy in loads + [kv_load]:
         copy.start()
-    lax.fori_loop(0, STEPS, greet, 0)
     for copy in loads:
         copy.wait()
 
@@ -133,7 +140,8 @@
                         jnp.concatenate(heads, axis=0).astype(bf16)
                     )
 
-    pl.semaphore_wait(barrier, 2 * STEPS)
+    pl.semaphore_wait(barrier, 16)
+    tell(second_stage)
 
     pack(0, s)
     self_copy = pltpu.make_async_copy(send.at[r], recv.at[r], self_sem)
@@ -143,8 +151,8 @@
     )
     pair_copy.start()
 
-    def ship(step, carry):
-        slot = target(step)
+    def ship(step, dz, dy, dx):
+        slot = target(dz, dy, dx)
         pack(step, slot)
         for row in range(2):
             pltpu.make_async_remote_copy(
@@ -155,9 +163,31 @@
                 device_id={"slot": slot, "row": row},
                 device_id_type=MESH,
             ).start()
-        return carry
-
-    lax.fori_loop(1, STEPS, ship, 0)
+
+    def ship_one(j, carry):
+        ship(2 * j - 1, j, 0, 0)
+        ship(2 * j, 0, j, 0)
+        return carry
+
+    def ship_two(j, carry):
+        step = 5 * j + 3
+        ship(step, j, 0, 1)
+        ship(step + 1, 0, j, 1)
+        for n in range(3):
+            ship(step + 2 + n, j, 1 + (j + n) % 3, 0)
+        return carry
+
+    def ship_three(m, carry):
+        ship(23 + m, 1 + m // 3, 1 + (m // 3 + m) % 3, 1)
+        return carry
+
+    lax.fori_loop(1, 4, ship_one, 0)
+    ship(7, 0, 0, 1)
+    pl.semaphore_wait(second_stage, 7)
+    tell(third_stage)
+    lax.fori_loop(1, 4, ship_two, 0)
+    pl.semaphore_wait(third_stage, 7)
+    lax.fori_loop(0, 9, ship_three, 0)
 
     hid_load.wait()
     for copy in w_loads[:3]:
@@ -237,9 +267,8 @@
     tile_row = lax.broadcasted_iota(i32, (TOK, KEYS), 0)
 
     def attend(n, done=None):
-        inner = src >> 1
-        b, cc = n % 4, n // 4
-        dz, dy, dx = inner, (inner + b) & 3, (inner + b + cc) & 1
+        code = steps_v[n : n + 1, :]
+        dz, dy, dx = code >> 4, (code >> 2) & 3, code & 1
         source = ((((z - src_sign * dz + 4) & 3) * NY + ((y - src_sign * dy + 4) & 3)) * NX + ((x + dx) & 1)) * 2 + src_row
         here = owner_sel[...] == source
         first = jnp.min(jnp.where(here, tile_row, FAR), axis=0, keepdims=True)
@@ -335,15 +364,17 @@
 ):
     freq = (ROPE_BASE ** (-2.0 * np.arange(HEAD // 2, dtype=np.float32) / HEAD)).astype(np.float32)
     freq = jnp.asarray(np.concatenate([freq, freq])[None, :])
+    steps = np.repeat([dz * 16 + dy * 4 + dx for dz, dy, dx in send_order()], 2 * MSG).reshape(CHUNKS, KEYS)
+    steps = jnp.asarray(steps, i32)
     dma = pltpu.SemaphoreType.DMA
     operands = (
         hidden, w_query, key_weight, value_weight, w_out, kv_store,
-        stretch_offset.reshape(64, 128), tile_stretch, slot_count, recomp_pos, freq,
+        stretch_offset.reshape(64, 128), tile_stretch, slot_count, recomp_pos, freq, steps,
     )
     return pl.pallas_call(
         kernel,
         out_shape=jax.ShapeDtypeStruct((1, 64, 2048), bf16),
-        in_specs=[pl.BlockSpec(memory_space=pltpu.HBM)] * 11,
+        in_specs=[pl.BlockSpec(memory_space=pltpu.HBM)] * 12,
         out_specs=pl.BlockSpec(memory_space=pltpu.VMEM),
         scratch_shapes=[
             pltpu.VMEM((TOK, 2048), bf16),
@@ -357,6 +388,7 @@
             pltpu.SMEM((32,), i32),
             pltpu.VMEM((1, 128), i32),
             pltpu.VMEM((1, 128), f32),
+            pltpu.VMEM((CHUNKS, KEYS), i32),
             pltpu.VMEM((2 * STEPS, 2, MSG, 256), bf16),
             pltpu.VMEM((2 * STEPS, 2, MSG, 256), bf16),
             pltpu.VMEM((STEPS, HEAD), i32),
@@ -378,8 +410,9 @@
             pltpu.VMEM((TOK, 2048), f32),
             pltpu.VMEM((8, 64, 256), bf16),
             pltpu.VMEM((8, 64, 256), bf16),
-            dma((2,)), dma((6,)), dma(()), dma((4,)), dma(()), dma(()), dma((CHUNKS,)),
+            dma((2,)), dma((7,)), dma(()), dma((4,)), dma(()), dma(()), dma((CHUNKS,)),
             dma(()), dma(()), dma(()), dma(()), dma((4,)), dma((4,)), dma((8,)), dma((8,)),
+            pltpu.SemaphoreType.REGULAR, pltpu.SemaphoreType.REGULAR,
         ],
         compiler_params=pltpu.CompilerParams(
             collective_id=0, has_side_effects=True, vmem_limit_bytes=44 << 20

time: 48.6 us -> 47.3 us (0.973)
  Pallas kernels: 47.8 us -> 46.4 us
    pallas_call x1, Pallas kernels: 47.8 us -> 46.4 us  [on_device(): pl.pallas_call(kernel, out_shape=jax.ShapeDtypeStruct((1, 64, 2048), bf16...]
where the time goes in v3:
time: 47.3 us; the launch traced here: 47.1 us
  Pallas kernels  46.4 us (98%)
  local copies, waits for them, and re-layouts  0.71 us (2%)
    pallas_call x1, Pallas kernels, on_device(): pl.pallas_call(kernel, out_shape=jax.ShapeDtypeStruct((1, 64, 2048), bf16...  46.4 us

profile of v3, /device:TPU:1, one launch (start us, length us, event | category | flops | bytes accessed | tf_op | source)
XLA Modules:
  0.0 47.1 jit_solution(16967754436456724734)
XLA Ops:
  0.0 46.4 %joined_attention.1 = bf16[1,64,2048]{2,1,0:T(8,128)(2,1)S(1)} custom-call(bf16[1,128,2048]{2,1,0:T(8,128)(2,1)} %hidden.1, bf16[2048,2048]{1,0:T(8,128)(2,1)} %w_query.1, bf16[2048,512]{1,0:T(8,128)(2,1)} %key_weight.1, bf16[2048,512]{1,0:T(8,128)(2,1)} %value_weight.1, bf16[2048,2048]{1,0:T(8,128)(2,1)} %w_out.1, bf16[128,2,8,512]{3,2,1,0:T(8,128)(2,1)} %kv_store.1, ...), custom_call_target="tpu_custom_call" | custom-call | tf_op jit(solution)/shard_map/joined_attention/pallas_call | solution.py:374
  46.4 0.7 %copy.14 = bf16[1,64,2048]{2,1,0:T(8,128)(2,1)} copy(bf16[1,64,2048]{2,1,0:T(8,128)(2,1)S(1)} %joined_attention.1) | data formatting | bytes 524288

commit v4 on v3

--- a/solution.py
+++ b/solution.py
@@ -27,15 +27,22 @@
 
 
 def send_order():
-    order = [(0, 0, 0)]
+    order = [(0, 0, 0), (0, 0, 1)]
     for j in range(1, 4):
         order += [(j, 0, 0), (0, j, 0)]
-    order += [(0, 0, 1)]
     for j in range(1, 4):
-        order += [(j, 0, 1), (0, j, 1)] + [(j, 1 + (j + n) % 3, 0) for n in range(3)]
+        order += [(j, 0, 1), (0, j, 1)]
     for m in range(9):
-        order += [(1 + m // 3, 1 + (m // 3 + m) % 3, 1)]
+        order += [(*far(m), 1), (*flat(m), 0)]
     return order
+
+
+def far(m):
+    return 1 + (m + 1) % 3, 1 + (m // 3 + m + 2) % 3
+
+
+def flat(m):
+    return 1 + m % 3, 1 + (m // 3 + m) % 3
 
 
 def kernel(
@@ -165,29 +172,27 @@
             ).start()
 
     def ship_one(j, carry):
-        ship(2 * j - 1, j, 0, 0)
-        ship(2 * j, 0, j, 0)
+        ship(2 * j, j, 0, 0)
+        ship(2 * j + 1, 0, j, 0)
         return carry
 
     def ship_two(j, carry):
-        step = 5 * j + 3
-        ship(step, j, 0, 1)
-        ship(step + 1, 0, j, 1)
-        for n in range(3):
-            ship(step + 2 + n, j, 1 + (j + n) % 3, 0)
-        return carry
-
-    def ship_three(m, carry):
-        ship(23 + m, 1 + m // 3, 1 + (m // 3 + m) % 3, 1)
-        return carry
-
+        ship(2 * j + 6, j, 0, 1)
+        ship(2 * j + 7, 0, j, 1)
+        return carry
+
+    def ship_rest(m, carry):
+        ship(2 * m + 14, *far(m), 1)
+        ship(2 * m + 15, *flat(m), 0)
+        return carry
+
+    ship(1, 0, 0, 1)
     lax.fori_loop(1, 4, ship_one, 0)
-    ship(7, 0, 0, 1)
     pl.semaphore_wait(second_stage, 7)
     tell(third_stage)
     lax.fori_loop(1, 4, ship_two, 0)
     pl.semaphore_wait(third_stage, 7)
-    lax.fori_loop(0, 9, ship_three, 0)
+    lax.fori_loop(0, 9, ship_rest, 0)
 
     hid_load.wait()
     for copy in w_loads[:3]:

time: 47.3 us -> 46.3 us (0.979)
  Pallas kernels: 46.4 us -> 45.4 us
    pallas_call x1, Pallas kernels: 46.4 us -> 45.4 us  [on_device(): pl.pallas_call(kernel, out_shape=jax.ShapeDtypeStruct((1, 64, 2048), bf16...]
where the time goes in v4:
time: 46.3 us; the launch traced here: 46.1 us
  Pallas kernels  45.4 us (98%)
  local copies, waits for them, and re-layouts  0.71 us (2%)
    pallas_call x1, Pallas kernels, on_device(): pl.pallas_call(kernel, out_shape=jax.ShapeDtypeStruct((1, 64, 2048), bf16...  45.4 us

profile of v4, /device:TPU:1, one launch (start us, length us, event | category | flops | bytes accessed | tf_op | source)
XLA Modules:
  0.0 46.1 jit_solution(463238379075492552)
XLA Ops:
  0.0 45.4 %joined_attention.1 = bf16[1,64,2048]{2,1,0:T(8,128)(2,1)S(1)} custom-call(bf16[1,128,2048]{2,1,0:T(8,128)(2,1)} %hidden.1, bf16[2048,2048]{1,0:T(8,128)(2,1)} %w_query.1, bf16[2048,512]{1,0:T(8,128)(2,1)} %key_weight.1, bf16[2048,512]{1,0:T(8,128)(2,1)} %value_weight.1, bf16[2048,2048]{1,0:T(8,128)(2,1)} %w_out.1, bf16[128,2,8,512]{3,2,1,0:T(8,128)(2,1)} %kv_store.1, ...), custom_call_target="tpu_custom_call" | custom-call | tf_op jit(solution)/shard_map/joined_attention/pallas_call | solution.py:379
  45.4 0.7 %copy.14 = bf16[1,64,2048]{2,1,0:T(8,128)(2,1)} copy(bf16[1,64,2048]{2,1,0:T(8,128)(2,1)S(1)} %joined_attention.1) | data formatting | bytes 524288

commit v5 on v4

--- a/solution.py
+++ b/solution.py
@@ -38,7 +38,7 @@
 
 
 def far(m):
-    return 1 + (m + 1) % 3, 1 + (m // 3 + m + 2) % 3
+    return 1 + (2 * m + 1) % 3, 1 + (m // 3 + m + 2) % 3
 
 
 def flat(m):
@@ -331,12 +331,6 @@
     def out_cols(n):
         return pl.ds(pl.multiple_of(n * 256, 256), 256)
 
-    def first_half(n, carry):
-        rows = pl.ds(pl.multiple_of(r * 1024, 1024), 1024)
-        o_acc[:, out_cols(n)] = jnp.dot(att[r], wo[rows, out_cols(n)], preferred_element_type=f32)
-        return carry
-
-    lax.fori_loop(0, 8, first_half, 0)
     att_copy(0).wait()
 
     def o_copy(n):
@@ -344,15 +338,16 @@
             o_send.at[n], o_recv.at[n], o_ssem.at[n], o_rsem.at[n], device_id={"col": 1 - c}, device_id_type=MESH
         )
 
-    def second_half(n, carry):
-        rows = pl.ds(pl.multiple_of((1 - r) * 1024, 1024), 1024)
-        o_acc[:, out_cols(n)] += jnp.dot(att[1 - r], wo[rows, out_cols(n)], preferred_element_type=f32)
+    def out_project(n, carry):
+        o_acc[:, out_cols(n)] = jnp.dot(att[0], wo[:1024, out_cols(n)], preferred_element_type=f32) + jnp.dot(
+            att[1], wo[1024:, out_cols(n)], preferred_element_type=f32
+        )
         o_send[n] = o_acc[pl.ds(pl.multiple_of((1 - c) * 64, 64), 64), out_cols(n)].astype(bf16)
         o_copy(n).start()
         return carry
 
     own_rows = pl.ds(pl.multiple_of(c * 64, 64), 64)
-    lax.fori_loop(0, 8, second_half, 0)
+    lax.fori_loop(0, 8, out_project, 0)
 
     def finish(n, carry):
         o_copy(n).wait()

time: 46.3 us -> 44.7 us (0.965)
  Pallas kernels: 45.4 us -> 43.9 us
    pallas_call x1, Pallas kernels: 45.4 us -> 43.9 us  [on_device(): pl.pallas_call(kernel, out_shape=jax.ShapeDtypeStruct((1, 64, 2048), bf16...]
where the time goes in v5:
time: 44.7 us; the launch traced here: 44.6 us
  Pallas kernels  43.9 us (98%)
  local copies, waits for them, and re-layouts  0.71 us (2%)
    pallas_call x1, Pallas kernels, on_device(): pl.pallas_call(kernel, out_shape=jax.ShapeDtypeStruct((1, 64, 2048), bf16...  43.9 us

profile of v5, /device:TPU:1, one launch (start us, length us, event | category | flops | bytes accessed | tf_op | source)
XLA Modules:
  0.0 44.6 jit_solution(606101721452846509)
XLA Ops:
  0.0 43.9 %joined_attention.1 = bf16[1,64,2048]{2,1,0:T(8,128)(2,1)S(1)} custom-call(bf16[1,128,2048]{2,1,0:T(8,128)(2,1)} %hidden.1, bf16[2048,2048]{1,0:T(8,128)(2,1)} %w_query.1, bf16[2048,512]{1,0:T(8,128)(2,1)} %key_weight.1, bf16[2048,512]{1,0:T(8,128)(2,1)} %value_weight.1, bf16[2048,2048]{1,0:T(8,128)(2,1)} %w_out.1, bf16[128,2,8,512]{3,2,1,0:T(8,128)(2,1)} %kv_store.1, ...), custom_call_target="tpu_custom_call" | custom-call | tf_op jit(solution)/shard_map/joined_attention/pallas_call | solution.py:374
  43.9 0.7 %copy.14 = bf16[1,64,2048]{2,1,0:T(8,128)(2,1)} copy(bf16[1,64,2048]{2,1,0:T(8,128)(2,1)S(1)} %joined_attention.1) | data formatting | bytes 524288

commit v6 on v5

--- a/solution.py
+++ b/solution.py
@@ -29,7 +29,7 @@
 def send_order():
     order = [(0, 0, 0), (0, 0, 1)]
     for j in range(1, 4):
-        order += [(j, 0, 0), (0, j, 0)]
+        order += [(4 - j, 0, 0), (0, j, 0)]
     for j in range(1, 4):
         order += [(j, 0, 1), (0, j, 1)]
     for m in range(9):
@@ -125,8 +125,6 @@
     id_copy.start()
     id_copy.wait()
     kv_load.wait()
-    for copy in [hid_load] + w_loads:
-        copy.start()
 
     def pack(step, slot):
         for b in range(2):
@@ -172,7 +170,7 @@
             ).start()
 
     def ship_one(j, carry):
-        ship(2 * j, j, 0, 0)
+        ship(2 * j, 4 - j, 0, 0)
         ship(2 * j + 1, 0, j, 0)
         return carry
 
@@ -194,6 +192,8 @@
     pl.semaphore_wait(third_stage, 7)
     lax.fori_loop(0, 9, ship_rest, 0)
 
+    for copy in [hid_load] + w_loads:
+        copy.start()
     hid_load.wait()
     for copy in w_loads[:3]:
         copy.wait()

time: 44.7 us -> 44.7 us (level)
  no operation moved by 1% of the time
where the time goes in v6:
time: 44.7 us; the launch traced here: 44.6 us
  Pallas kernels  43.9 us (98%)
  local copies, waits for them, and re-layouts  0.71 us (2%)
    pallas_call x1, Pallas kernels, on_device(): pl.pallas_call(kernel, out_shape=jax.ShapeDtypeStruct((1, 64, 2048), bf16...  43.9 us

profile of v6, /device:TPU:1, one launch (start us, length us, event | category | flops | bytes accessed | tf_op | source)
XLA Modules:
  0.0 44.6 jit_solution(8310937992375046963)
XLA Ops:
  0.0 43.9 %joined_attention.1 = bf16[1,64,2048]{2,1,0:T(8,128)(2,1)S(1)} custom-call(bf16[1,128,2048]{2,1,0:T(8,128)(2,1)} %hidden.1, bf16[2048,2048]{1,0:T(8,128)(2,1)} %w_query.1, bf16[2048,512]{1,0:T(8,128)(2,1)} %key_weight.1, bf16[2048,512]{1,0:T(8,128)(2,1)} %value_weight.1, bf16[2048,2048]{1,0:T(8,128)(2,1)} %w_out.1, bf16[128,2,8,512]{3,2,1,0:T(8,128)(2,1)} %kv_store.1, ...), custom_call_target="tpu_custom_call" | custom-call | tf_op jit(solution)/shard_map/joined_attention/pallas_call | solution.py:374
  43.9 0.7 %copy.14 = bf16[1,64,2048]{2,1,0:T(8,128)(2,1)} copy(bf16[1,64,2048]{2,1,0:T(8,128)(2,1)S(1)} %joined_attention.1) | data formatting | bytes 524288
